TPU v7x, 512 devices: a whole 4x4x16 slice. The times are simulated.
512 devices in a mesh: inb: 16 (over y, z_lo), hid: 32 (over z_hi, x, core).
Axes of the slice: x: 4, y: 4, z: 16 (z_hi: 4, z_lo: 4; z = z_hi * 4 + z_lo), core: 2. Of those that a mesh axis runs over, the one named last changes fastest.
Arguments:
- activations: bfloat16 [2, 512, 16384], P(None, 'hid', 'inb'), may hold values from -40 to 40
- out_grads: bfloat16 [2, 512, 32768], P(None, 'inb', 'hid'), may hold values from -1 to 1
- basis_in: bfloat16 [16384, 1024], P('inb', 'hid'), may hold values from -0.1875 to 0.1875
- basis_out: bfloat16 [32768, 1024], P('hid', 'inb'), may hold values from -0.1875 to 0.1875
Outputs:
- precond: bfloat16 [16384, 32768], P('inb', 'hid')
All inputs are finite; a program needn't handle non-finite values.
Results may differ from a plain program's by a relative error of at most 0.0058.
Values may be sent and summed in bfloat16 or wider, within the bound.
A program may use at most 64 MiB of HBM per device.

v0:
```python
import jax
import jax.numpy as jnp
from jax import lax
from jax.sharding import PartitionSpec as P

damping = 0.1


def square_round(values):
    widened = values.astype(jnp.float32)
    return (widened * widened).astype(jnp.bfloat16)


def contract_tokens(left_side, right_side):
    return lax.dot_general(
        left_side, right_side, (((0, 1), (0, 1)), ((), ())), preferred_element_type=jnp.float32
    )


def on_device(activations, out_grads, basis_in, basis_out):
    micro_count = activations.shape[0]
    width_block = basis_in.shape[0]
    grads_flat = out_grads.reshape(-1, width_block)
    grads_rot = (
        jnp.dot(
            grads_flat,
            lax.all_gather(basis_out, "inb", axis=1, tiled=True),
            preferred_element_type=jnp.float32,
        )
        .astype(jnp.bfloat16)
        .reshape(out_grads.shape)
    )
    basis_whole = lax.all_gather(basis_in, "hid", axis=1, tiled=True)
    groups = [(number, number + 1) for number in range(micro_count)]
    grad_sum = jnp.zeros((width_block, width_block), jnp.float32)
    fisher_sum = jnp.zeros((width_block, width_block), jnp.float32)
    for lower_mb, upper_mb in groups:
        grads_full = lax.all_gather(grads_rot[lower_mb:upper_mb], "inb", axis=1, tiled=True)
        grads_squared = square_round(grads_full)
        plain_rows = lax.all_gather(activations[lower_mb:upper_mb], "hid", axis=1, tiled=True)
        rotated = (
            jnp.dot(
                plain_rows.reshape(-1, width_block), basis_whole, preferred_element_type=jnp.float32
            )
            .astype(jnp.bfloat16)
            .reshape(plain_rows.shape)
        )
        grad_sum = grad_sum + contract_tokens(rotated, grads_full)
        fisher_sum = fisher_sum + contract_tokens(square_round(rotated), grads_squared)
    return (grad_sum / (fisher_sum + damping)).astype(jnp.bfloat16)


def solution(mesh):
    return jax.shard_map(
        on_device,
        mesh=mesh,
        in_specs=(P(None, "hid", "inb"), P(None, "inb", "hid"), P("inb", "hid"), P("hid", "inb")),
        out_specs=P("inb", "hid"),
        check_vma=False,
    )
```

profile of v0, /device:TPU:2, one launch (start us, length us, event | category | flops | bytes accessed | tf_op | source)
XLA Modules:
  0.0 509.5 jit_solution(13084223138114623987)
XLA Ops:
  6.5 0.0 copy-start
  6.5 0.0 all-gather.13.cloned.1.call-start
  6.5 0.7 all-gather.13.cloned.1.call-update
  7.3 0.0 all-gather.15.cloned.1.call-start
  7.3 1.4 fusion.4
  8.7 0.0 all-gather.15.cloned.1.call-update
  8.7 0.0 all-gather.11.cloned.1.call-start
  8.8 0.7 all-gather.11.cloned.1.call-update
  9.5 0.0 all-gather.9.cloned.1.call-start
  9.5 0.5 all-gather.9.cloned.1.call-update
  10.0 0.0 all-gather.17.cloned.1.call-start
  10.1 95.8 %all-gather.13.cloned.1.call-done = bf16[1024,1024]{0,1:T(8,128)(2,1)} async-done(((bf16[1024,64]{0,1:T(8,128)(2,1)}), bf16[1024,1024]{0,1:T(8,128)(2,1)}) %all-gather.13.cloned.1.call-update) | async-done | bytes 2097168 | tf_op jit(solution)/shard_map/all_gather | solution.py:27
  105.8 0.0 copy-done
  105.8 2.3 convolution_convert_fusion.2
  108.2 0.7 fusion.3
  108.9 0.0 all-gather.17.cloned.1.call-update
  108.9 0.0 all-gather.19.cloned.1.call-start
  108.9 0.5 all-gather.19.cloned.1.call-update
  109.5 68.9 %all-gather.15.cloned.1.call-done = bf16[1,512,1024]{2,1,0:T(8,128)(2,1)} async-done(((bf16[1,16,1024]{2,1,0:T(8,128)(2,1)}), bf16[1,512,1024]{2,1,0:T(8,128)(2,1)}) %all-gather.15.cloned.1.call-update) | async-done | bytes 1048592 | tf_op jit(solution)/shard_map/all_gather | solution.py:40
  178.4 76.6 %all-gather.11.cloned.1.call-done = bf16[1024,1024]{0,1:T(8,128)(2,1)} async-done(((bf16[1024,32]{0,1:T(8,128)(2,1)}), bf16[1024,1024]{0,1:T(8,128)(2,1)}) %all-gather.11.cloned.1.call-update) | async-done | bytes 2097168 | tf_op jit(solution)/shard_map/all_gather | solution.py:33
  254.9 3.2 convolution_convert_fusion
  258.2 64.8 %all-gather.9.cloned.1.call-done = bf16[1,512,1024]{2,1,0:T(8,128)(2,1)} async-done(((bf16[1,16,1024]{2,1,0:T(8,128)(2,1)}), bf16[1,512,1024]{2,1,0:T(8,128)(2,1)}) %all-gather.9.cloned.1.call-update) | async-done | bytes 1048592 | tf_op jit(solution)/shard_map/all_gather | solution.py:40
  322.9 3.2 convolution_convert_fusion.1
  326.1 80.6 %all-gather.17.cloned.1.call-done = bf16[512,1024]{1,0:T(8,128)(2,1)} async-done(((bf16[32,1024]{1,0:T(8,128)(2,1)}), bf16[512,1024]{1,0:T(8,128)(2,1)}) %all-gather.17.cloned.1.call-update) | async-done | bytes 1048592 | tf_op jit(solution)/shard_map/all_gather | solution.py:38
  406.7 0.0 copy-start.2
  406.7 4.5 fusion
  411.2 0.0 copy-done.2
  411.2 3.3 fusion.5
  414.6 79.8 %all-gather.19.cloned.1.call-done = bf16[512,1024]{1,0:T(8,128)(2,1)} async-done(((bf16[32,1024]{1,0:T(8,128)(2,1)}), bf16[512,1024]{1,0:T(8,128)(2,1)}) %all-gather.19.cloned.1.call-update) | async-done | bytes 1048592 | tf_op jit(solution)/shard_map/all_gather | solution.py:38
  494.3 0.0 copy-start.1
  494.3 0.0 copy-start.3
  494.3 2.7 fusion.6
  497.0 0.0 copy-done.1
  497.0 0.1 copy-done.3
  497.1 5.5 %divide_convert_fusion = bf16[1024,1024]{1,0:T(8,128)(2,1)} fusion(f32[1024,1024]{1,0:T(8,128)} %fusion, f32[1024,1024]{1,0:T(8,128)S(1)} %copy-done.1, f32[1024,1024]{1,0:T(8,128)S(1)} %fusion.6, bf16[512,1024]{1,0:T(8,128)(2,1)S(1)} %convolution_convert_fusion, bf16[512,1024]{1,0:T(8,128)(2,1)S(1)} %copy-done.3), kind=kOutput, calls=%fused_computation | convolution fusion | flops 1082130432 | bytes 16777216 | tf_op jit(solution)/shard_map/dot_general | solution.py:15
Async XLA Ops:
  6.5 99.3 %copy-start = (bf16[2,32,1024]{2,1,0:T(8,128)(2,1)S(1)}, bf16[2,32,1024]{2,1,0:T(8,128)(2,1)}, u32[]{:S(2)}) copy-start(bf16[2,32,1024]{2,1,0:T(8,128)(2,1)} %param.5) | copy-start | bytes 393220
  6.5 99.3 %all-gather.13.cloned.1.call-start = ((), (), s32[]{:S(2)}) async-start(), calls=%async_computation.2 | async-start | bytes 2228224 | tf_op jit(solution)/shard_map/all_gather | solution.py:27
  7.3 171.1 %all-gather.15.cloned.1.call-start = ((), (), s32[]{:S(2)}) async-start(), calls=%async_computation.3 | async-start | bytes 1081344 | tf_op jit(solution)/shard_map/all_gather | solution.py:40
  8.7 246.2 %all-gather.11.cloned.1.call-start = ((), (), s32[]{:S(2)}) async-start(), calls=%async_computation.1 | async-start | bytes 2162688 | tf_op jit(solution)/shard_map/all_gather | solution.py:33
  9.5 313.4 %all-gather.9.cloned.1.call-start = ((), (), s32[]{:S(2)}) async-start(), calls=%async_computation | async-start | bytes 1081344 | tf_op jit(solution)/shard_map/all_gather | solution.py:40
  10.0 396.6 %all-gather.17.cloned.1.call-start = ((), (), s32[]{:S(2)}) async-start(), calls=%async_computation.4 | async-start | bytes 1114112 | tf_op jit(solution)/shard_map/all_gather | solution.py:38
  108.9 385.4 %all-gather.19.cloned.1.call-start = ((), (), s32[]{:S(2)}) async-start(), calls=%async_computation.5 | async-start | bytes 1114112 | tf_op jit(solution)/shard_map/all_gather | solution.py:38
  406.7 4.6 copy-start.2
  494.3 2.7 copy-start.1
  494.3 2.8 copy-start.3
Sparse Core Ops, SparseCore 0:
  9.4 96.3 all-gather.12
  109.0 69.3 all-gather.14
  181.5 73.3 all-gather.10
  257.9 64.9 all-gather.8
  324.8 81.8 all-gather.16
  408.6 85.6 all-gather.18
where the time goes:
time: 510 us; the launch traced here: 509 us
  waiting for transfers between devices  469 us (92%)
  matrix products  24.8 us (5%)
  between operations  13.5 us (3%)
    all_gather x2, waiting for transfers between devices, on_device(): lax.all_gather(grads_rot[lower_mb:upper_mb], 'inb', axis=1, tiled=True)  160 us
    all_gather x2, waiting for transfers between devices, on_device(): lax.all_gather(activations[lower_mb:upper_mb], 'hid', axis=1, tiled=True)  134 us
    all_gather x1, waiting for transfers between devices, on_device(): lax.all_gather(basis_out, 'inb', axis=1, tiled=True)  95.8 us
    all_gather x1, waiting for transfers between devices, on_device(): basis_whole = lax.all_gather(basis_in, 'hid', axis=1, tiled=True)  76.6 us
    dot_general x4, matrix products, contract_tokens(): lax.dot_general(left_side, right_side, (((0, 1), (0, 1)), ((), ())), pref...  16 us
  transfers between devices with their start and end apart: 6, of which 6 were waited for; matrix products, arithmetic and copies ran while one was open for 4% of the time, Pallas kernels for 0%

commit v1 on v0

--- a/solution.py
+++ b/solution.py
@@ -24,7 +24,9 @@
     grads_rot = (
         jnp.dot(
             grads_flat,
-            lax.all_gather(basis_out, "inb", axis=1, tiled=True),
+            jnp.concatenate(
+                lax.all_to_all(jnp.stack([basis_out] * lax.axis_size("inb")), "inb", 0, 0), axis=1
+            ),
             preferred_element_type=jnp.float32,
         )
         .astype(jnp.bfloat16)

time: 510 us -> 431 us (0.85)
  the two profiles are of different devices: /device:TPU:2 before, /device:TPU:4 now
where the time goes in v1:
time: 431 us
  waiting for transfers between devices  381 us (88%)
  matrix products  23.2 us (5%)
  between operations  13.2 us (3%)
  starting transfers between devices  8.97 us (2%)
    all_gather x2, waiting for transfers between devices, on_device(): lax.all_gather(grads_rot[lower_mb:upper_mb], 'inb', axis=1, tiled=True)  161 us
    all_gather x2, waiting for transfers between devices, on_device(): lax.all_gather(activations[lower_mb:upper_mb], 'hid', axis=1, tiled=True)  91.4 us
    all_gather x1, waiting for transfers between devices, on_device(): basis_whole = lax.all_gather(basis_in, 'hid', axis=1, tiled=True)  77 us
    all_to_all x1, waiting for transfers between devices, on_device(): lax.all_to_all(jnp.stack([basis_out] * lax.axis_size('inb')), 'inb', 0, 0)  50.1 us
    dot_general x4, matrix products, contract_tokens(): lax.dot_general(left_side, right_side, (((0, 1), (0, 1)), ((), ())), pref...  16 us
    all_to_all x1, starting transfers between devices, on_device(): lax.all_to_all(jnp.stack([basis_out] * lax.axis_size('inb')), 'inb', 0, 0)  8.77 us
  transfers between devices with their start and end apart: 6, of which 6 were waited for; matrix products, arithmetic and copies ran while one was open for 4% of the time, Pallas kernels for 0%

profile of v1, /device:TPU:4, one launch (start us, length us, event | category | flops | bytes accessed | tf_op | source)
XLA Modules:
  0.0 430.5 jit_solution(1951010366498962563)
XLA Ops:
  6.5 0.0 copy-start
  6.5 2.5 stack.2
  9.1 0.0 copy-start.4
  9.1 8.8 %all-to-all-start = ((bf16[16,1024,64]{1,2,0:T(8,128)(2,1)}), bf16[16,1024,64]{1,2,0:T(8,128)(2,1)S(1)}, u32[]{:S(2)}, u32[]{:S(2)}) async-start(bf16[16,1024,64]{1,2,0:T(8,128)(2,1)} %stack.2), calls=%async_computation | async-start | bytes 4194304 | tf_op jit(solution)/shard_map/all_to_all | solution.py:28
  17.8 0.0 all-gather.12.cloned.1.call-start
  17.9 0.0 copy-done.4
  17.9 0.6 fusion.4
  18.5 0.0 all-gather.12.cloned.1.call-update
  18.6 0.0 all-gather.10.cloned.1.call-start
  18.6 0.7 all-gather.10.cloned.1.call-update
  19.3 0.0 all-gather.8.cloned.1.call-start
  19.4 0.7 all-gather.8.cloned.1.call-update
  20.1 0.0 all-gather.14.cloned.1.call-start
  20.1 50.1 %all-to-all-done = bf16[16,1024,64]{1,2,0:T(8,128)(2,1)S(1)} async-done(((bf16[16,1024,64]{1,2,0:T(8,128)(2,1)}), bf16[16,1024,64]{1,2,0:T(8,128)(2,1)S(1)}, u32[]{:S(2)}, u32[]{:S(2)}) %all-to-all-start) | async-done | bytes 2097184 | tf_op jit(solution)/shard_map/all_to_all | solution.py:28
  70.2 0.0 copy-done
  70.2 0.8 convolution_convert_fusion.2
  71.0 0.7 fusion.3
  71.6 0.0 all-gather.14.cloned.1.call-update
  71.6 0.0 all-gather.16.cloned.1.call-start
  71.7 0.5 all-gather.16.cloned.1.call-update
  72.2 26.9 %all-gather.12.cloned.1.call-done = bf16[1,512,1024]{2,1,0:T(8,128)(2,1)} async-done(((bf16[1,16,1024]{2,1,0:T(8,128)(2,1)}), bf16[1,512,1024]{2,1,0:T(8,128)(2,1)}) %all-gather.12.cloned.1.call-update) | async-done | bytes 1048592 | tf_op jit(solution)/shard_map/all_gather | solution.py:42
  99.1 77.0 %all-gather.10.cloned.1.call-done = bf16[1024,1024]{0,1:T(8,128)(2,1)} async-done(((bf16[1024,32]{0,1:T(8,128)(2,1)}), bf16[1024,1024]{0,1:T(8,128)(2,1)}) %all-gather.10.cloned.1.call-update) | async-done | bytes 2097168 | tf_op jit(solution)/shard_map/all_gather | solution.py:35
  176.1 3.2 convolution_convert_fusion
  179.3 64.5 %all-gather.8.cloned.1.call-done = bf16[1,512,1024]{2,1,0:T(8,128)(2,1)} async-done(((bf16[1,16,1024]{2,1,0:T(8,128)(2,1)}), bf16[1,512,1024]{2,1,0:T(8,128)(2,1)}) %all-gather.8.cloned.1.call-update) | async-done | bytes 1048592 | tf_op jit(solution)/shard_map/all_gather | solution.py:42
  243.8 3.2 convolution_convert_fusion.1
  247.0 80.9 %all-gather.14.cloned.1.call-done = bf16[512,1024]{1,0:T(8,128)(2,1)} async-done(((bf16[32,1024]{1,0:T(8,128)(2,1)}), bf16[512,1024]{1,0:T(8,128)(2,1)}) %all-gather.14.cloned.1.call-update) | async-done | bytes 1048592 | tf_op jit(solution)/shard_map/all_gather | solution.py:40
  327.8 0.0 copy-start.2
  327.8 4.6 %fusion.5 = f32[1024,1024]{1,0:T(8,128)} fusion(bf16[512,1024]{1,0:T(8,128)(2,1)S(1)} %convolution_convert_fusion.1, bf16[512,1024]{1,0:T(8,128)(2,1)} %all-gather.14.cloned.1.call-done), kind=kOutput, calls=%fused_computation.13 | convolution fusion | flops 1073741824 | bytes 6291456 | tf_op jit(solution)/shard_map/dot_general | solution.py:15
  332.4 0.0 copy-done.2
  332.5 3.2 fusion
  335.7 80.0 %all-gather.16.cloned.1.call-done = bf16[512,1024]{1,0:T(8,128)(2,1)} async-done(((bf16[32,1024]{1,0:T(8,128)(2,1)}), bf16[512,1024]{1,0:T(8,128)(2,1)}) %all-gather.16.cloned.1.call-update) | async-done | bytes 1048592 | tf_op jit(solution)/shard_map/all_gather | solution.py:40
  415.7 0.0 copy-start.1
  415.7 0.0 copy-start.3
  415.7 2.7 fusion.6
  418.3 0.0 copy-done.1
  418.3 0.1 copy-done.3
  418.5 5.5 %divide_convert_fusion = bf16[1024,1024]{1,0:T(8,128)(2,1)} fusion(f32[1024,1024]{1,0:T(8,128)} %fusion, f32[1024,1024]{1,0:T(8,128)S(1)} %copy-done.1, f32[1024,1024]{1,0:T(8,128)S(1)} %fusion.6, bf16[512,1024]{1,0:T(8,128)(2,1)S(1)} %convolution_convert_fusion, bf16[512,1024]{1,0:T(8,128)(2,1)S(1)} %copy-done.3), kind=kOutput, calls=%fused_computation | convolution fusion | flops 1082130432 | bytes 16777216 | tf_op jit(solution)/shard_map/dot_general | solution.py:15
Async XLA Ops:
  6.5 63.7 %copy-start = (bf16[2,32,1024]{2,1,0:T(8,128)(2,1)S(1)}, bf16[2,32,1024]{2,1,0:T(8,128)(2,1)}, u32[]{:S(2)}) copy-start(bf16[2,32,1024]{2,1,0:T(8,128)(2,1)} %param.5) | copy-start | bytes 393220
  9.1 8.8 %copy-start.4 = (bf16[2,16,1024]{2,1,0:T(8,128)(2,1)S(1)}, bf16[2,16,1024]{2,1,0:T(8,128)(2,1)}, u32[]{:S(2)}) copy-start(bf16[2,16,1024]{2,1,0:T(8,128)(2,1)} %param.4) | copy-start | bytes 196612
  9.1 61.1 %all-to-all-start = ((bf16[16,1024,64]{1,2,0:T(8,128)(2,1)}), bf16[16,1024,64]{1,2,0:T(8,128)(2,1)S(1)}, u32[]{:S(2)}, u32[]{:S(2)}) async-start(bf16[16,1024,64]{1,2,0:T(8,128)(2,1)} %stack.2), calls=%async_computation | async-start | bytes 4194304 | tf_op jit(solution)/shard_map/all_to_all | solution.py:28
  17.8 81.3 %all-gather.12.cloned.1.call-start = ((), (), s32[]{:S(2)}) async-start(), calls=%async_computation.3 | async-start | bytes 1081344 | tf_op jit(solution)/shard_map/all_gather | solution.py:42
  18.6 157.5 %all-gather.10.cloned.1.call-start = ((), (), s32[]{:S(2)}) async-start(), calls=%async_computation.2 | async-start | bytes 2162688 | tf_op jit(solution)/shard_map/all_gather | solution.py:35
  19.3 224.5 %all-gather.8.cloned.1.call-start = ((), (), s32[]{:S(2)}) async-start(), calls=%async_computation.1 | async-start | bytes 1081344 | tf_op jit(solution)/shard_map/all_gather | solution.py:42
  20.1 307.8 %all-gather.14.cloned.1.call-start = ((), (), s32[]{:S(2)}) async-start(), calls=%async_computation.4 | async-start | bytes 1114112 | tf_op jit(solution)/shard_map/all_gather | solution.py:40
  71.6 344.0 %all-gather.16.cloned.1.call-start = ((), (), s32[]{:S(2)}) async-start(), calls=%async_computation.5 | async-start | bytes 1114112 | tf_op jit(solution)/shard_map/all_gather | solution.py:40
  327.8 4.6 %copy-start.2 = (bf16[512,1024]{1,0:T(8,128)(2,1)S(1)}, bf16[512,1024]{1,0:T(8,128)(2,1)}, u32[]{:S(2)}) copy-start(bf16[512,1024]{1,0:T(8,128)(2,1)} %all-gather.14.cloned.1.call-done) | copy-start | bytes 3145732
  415.7 2.7 copy-start.1
  415.7 2.8 copy-start.3
Sparse Core Ops, SparseCore 0:
  21.8 77.2 all-gather.11
  102.2 73.8 all-gather.9
  179.2 64.4 all-gather.7
  245.7 82.0 all-gather.13
  329.8 85.8 all-gather.15
